TPU v7x, 256 devices: a whole 4x4x8 slice. The times are simulated.
256 devices in a mesh: row: 64 (over z, x, core), col: 4 (over y).
Axes of the slice: x: 4, y: 4, z: 8, core: 2. Of those that a mesh axis runs over, the one named last changes fastest.
Arguments:
- right_sides: float32 [4, 256, 128, 128], P(None, 'row'), may hold values from -6 to 6
- inverse_diag: float32 [4, 256, 128, 128], P(None, 'row', 'col'), may hold values from -1 to 2
- lower_blocks: float32 [3, 256, 16, 128, 128], P(None, 'row', None, 'col'), may hold values from -0.09375 to 0.09375
- depends_on: int32 [3, 256, 16], replicated, may hold values from 0 to 255, as said below
Outputs:
- solution: float32 [4, 256, 128, 128], P(None, 'row', 'col')
Inputs may be any that keep to these rules, and one draw needn't show every extreme that they name: `depends_on`: in each level, the supernodes of one device along row name the supernodes of any one device along row at most 2 times in all, and some pair of devices reaches 2 in every level.
All inputs are finite; a program needn't handle non-finite values.
Results may differ from a plain program's by a relative error of at most 0.0001.
Values sent between devices are 32-bit elements; how exact they have to be, the bound alone decides.
A program may use at most 64 MiB of HBM per device.

v0:
```python
import jax
import jax.numpy as jnp
from jax import lax
from jax.sharding import PartitionSpec as P

exact_mode = lax.Precision.HIGHEST


def fetch_blocks(previous, wanted):
    shard_rows = lax.all_gather(previous, "row", axis=0, tiled=True)
    chooser = (wanted[:, None] == jnp.arange(shard_rows.shape[0], dtype=jnp.int32)[None, :]).astype(
        jnp.float32
    )
    return jnp.einsum("en,nrk->erk", chooser, shard_rows, precision=exact_mode)


def return_terms(terms, wanted, local_count):
    owners = (
        jnp.arange(local_count * lax.axis_size("row"), dtype=jnp.int32)[:, None] == wanted[None, :]
    ).astype(jnp.float32)
    return lax.psum_scatter(
        jnp.einsum("me,erk->mrk", owners, terms, precision=exact_mode),
        "row",
        scatter_dimension=0,
        tiled=True,
    )


def forward_update(partial_value):
    return lax.psum(partial_value, "col")


def backward_solve(inverse_level, rest):
    partial_value = jnp.einsum("jab,jak->jbk", inverse_level, rest, precision=exact_mode)
    return lax.psum(partial_value, "col")


def on_device(right_sides, inverse_diag, lower_blocks, depends_on):
    levels, local_count, width, columns = right_sides.shape
    share = inverse_diag.shape[2]
    fan_in = lower_blocks.shape[2]
    my_row = lax.axis_index("row")
    my_col = lax.axis_index("col")
    entries = local_count * fan_in
    wanted_all = [
        lax.dynamic_slice_in_dim(
            depends_on[level_no], my_row * local_count, local_count, 0
        ).reshape(entries)
        for level_no in range(levels - 1)
    ]
    solved_here = [
        jnp.einsum("jab,jbk->jak", inverse_diag[0], right_sides[0], precision=exact_mode)
    ]
    for level_no in range(1, levels):
        picked = fetch_blocks(solved_here[-1], wanted_all[level_no - 1])
        partial_value = jnp.einsum(
            "jdba,jdbk->jak",
            lower_blocks[level_no - 1],
            picked.reshape(local_count, fan_in, share, columns),
            precision=exact_mode,
        )
        update = forward_update(partial_value)
        residual = right_sides[level_no] - update
        solved_here.append(
            jnp.einsum("jab,jbk->jak", inverse_diag[level_no], residual, precision=exact_mode)
        )
    full_sol = backward_solve(inverse_diag[levels - 1], solved_here[levels - 1])
    pieces = [lax.dynamic_slice_in_dim(full_sol, my_col * share, share, 1)]
    for level_no in range(levels - 2, -1, -1):
        terms = jnp.einsum(
            "jdba,jak->jdbk", lower_blocks[level_no], full_sol, precision=exact_mode
        ).reshape(entries, share, columns)
        returned = return_terms(terms, wanted_all[level_no], local_count)
        rest = solved_here[level_no] - returned
        full_sol = backward_solve(inverse_diag[level_no], rest)
        pieces.insert(0, lax.dynamic_slice_in_dim(full_sol, my_col * share, share, 1))
    return jnp.stack(pieces)


def solution(mesh):
    return jax.shard_map(
        on_device,
        mesh=mesh,
        in_specs=(
            P(None, "row", None, None),
            P(None, "row", "col", None),
            P(None, "row", None, "col", None),
            P(),
        ),
        out_specs=P(None, "row", "col", None),
        check_vma=False,
    )
```

profile of v0, /device:TPU:2, one launch (start us, length us, event | category | flops | bytes accessed | tf_op | source)
XLA Modules:
  0.0 1079.7 jit_solution(4726448590712107465)
XLA Ops:
  6.5 1.9 fusion.22
  8.6 0.8 fusion.67
  9.3 0.1 constant_dynamic-slice_fusion.6
  9.4 0.1 copy.27
  9.5 0.1 eq.85
  9.6 3.6 fusion.65
  13.2 77.8 %all-gather.4.cloned.1.call-done = f32[256,32,128]{2,1,0:T(8,128)} async-done(((f32[4,32,128]{2,1,0:T(8,128)}), f32[256,32,128]{2,1,0:T(8,128)}) %all-gather.4.cloned.1.call-update) | async-done | bytes 4194320 | tf_op jit(solution)/shard_map/all_gather | solution.py:10
  91.0 6.2 fusion.4
  97.2 3.0 convolution_bitcast_fusion.6
  100.3 0.8 fusion.66
  101.0 0.1 copy.70
  101.2 44.4 %all-reduce.8.cloned.1.call-done = f32[4,128,128]{1,2,0:T(8,128)} async-done(((f32[4,128,128]{1,2,0:T(8,128)}), f32[4,128,128]{1,2,0:T(8,128)}) %all-reduce.8.cloned.1.call-update) | async-done | bytes 262160 | tf_op jit(solution)/shard_map/psum | solution.py:30
  145.6 2.1 convolution_bitcast_fusion.8
  147.7 0.3 all-reduce.10.cloned.1.call-start
  148.0 0.1 constant_dynamic-slice_fusion.4
  148.1 0.1 copy.32
  148.2 0.1 eq.92
  148.3 78.8 %all-gather.6.cloned.1.call-done = f32[256,32,128]{2,1,0:T(8,128)} async-done(((f32[4,32,128]{2,1,0:T(8,128)}), f32[256,32,128]{2,1,0:T(8,128)}) %all-gather.6.cloned.1.call-update) | async-done | bytes 4194320 | tf_op jit(solution)/shard_map/all_gather | solution.py:10
  227.1 6.1 fusion.2
  233.2 3.0 convolution_bitcast_fusion.5
  236.3 0.1 copy.72
  236.4 45.2 %all-reduce.10.cloned.1.call-done = f32[4,128,128]{1,2,0:T(8,128)} async-done(((f32[4,128,128]{1,2,0:T(8,128)}), f32[4,128,128]{1,2,0:T(8,128)}) %all-reduce.10.cloned.1.call-update) | async-done | bytes 262160 | tf_op jit(solution)/shard_map/psum | solution.py:30
  281.6 2.1 convolution_bitcast_fusion.7
  283.7 0.4 all-reduce.12.cloned.1.call-start
  284.1 0.1 copy.37
  284.2 0.1 eq.99
  284.3 78.3 %all-gather.8.cloned.1.call-done = f32[256,32,128]{2,1,0:T(8,128)} async-done(((f32[4,32,128]{2,1,0:T(8,128)}), f32[256,32,128]{2,1,0:T(8,128)}) %all-gather.8.cloned.1.call-update) | async-done | bytes 4194320 | tf_op jit(solution)/shard_map/all_gather | solution.py:10
  362.6 6.1 fusion
  368.7 4.4 convolution_bitcast_fusion.4
  373.2 1.8 copy.74
  375.0 43.5 %all-reduce.12.cloned.1.call-done = f32[4,128,128]{1,2,0:T(8,128)} async-done(((f32[4,128,128]{1,2,0:T(8,128)}), f32[4,128,128]{1,2,0:T(8,128)}) %all-reduce.12.cloned.1.call-update) | async-done | bytes 262160 | tf_op jit(solution)/shard_map/psum | solution.py:30
  418.5 1.5 fusion.21
  420.1 1.3 convolution_bitcast_fusion.3
  421.4 0.6 reduce-scatter.4.cloned.1.call-start
  422.0 46.8 %all-reduce.14.cloned.1.call-done = f32[4,128,128]{1,2,0:T(8,128)} async-done(((f32[4,128,128]{1,2,0:T(8,128)}), f32[4,128,128]{1,2,0:T(8,128)}) %all-reduce.14.cloned.1.call-update) | async-done | bytes 262160 | tf_op jit(solution)/shard_map/psum | solution.py:35
  468.8 1.9 fusion.10
  470.8 2.3 fusion.16
  473.1 4.4 copy.45
  477.6 143.6 %reduce-scatter.4.cloned.1.call-done = f32[4,32,128]{2,1,0:T(8,128)} async-done(((f32[256,32,128]{2,1,0:T(8,128)}), f32[4,32,128]{2,1,0:T(8,128)}) %reduce-scatter.4.cloned.1.call-update) | async-done | bytes 65552 | tf_op jit(solution)/shard_map/reduce_scatter | solution.py:21
  621.1 2.1 convolution_bitcast_fusion.2
  623.3 0.2 reduce-scatter.6.cloned.1.call-start
  623.5 46.0 %all-reduce.16.cloned.1.call-done = f32[4,128,128]{1,2,0:T(8,128)} async-done(((f32[4,128,128]{1,2,0:T(8,128)}), f32[4,128,128]{1,2,0:T(8,128)}) %all-reduce.16.cloned.1.call-update) | async-done | bytes 262160 | tf_op jit(solution)/shard_map/psum | solution.py:35
  669.6 1.9 fusion.8
  671.5 2.3 fusion.14
  673.9 4.4 copy.49
  678.3 143.5 %reduce-scatter.6.cloned.1.call-done = f32[4,32,128]{2,1,0:T(8,128)} async-done(((f32[256,32,128]{2,1,0:T(8,128)}), f32[4,32,128]{2,1,0:T(8,128)}) %reduce-scatter.6.cloned.1.call-update) | async-done | bytes 65552 | tf_op jit(solution)/shard_map/reduce_scatter | solution.py:21
  821.8 2.1 convolution_bitcast_fusion.1
  824.0 0.3 reduce-scatter.8.cloned.1.call-start
  824.3 46.0 %all-reduce.18.cloned.1.call-done = f32[4,128,128]{1,2,0:T(8,128)} async-done(((f32[4,128,128]{1,2,0:T(8,128)}), f32[4,128,128]{1,2,0:T(8,128)}) %all-reduce.18.cloned.1.call-update) | async-done | bytes 262160 | tf_op jit(solution)/shard_map/psum | solution.py:35
  870.3 1.9 fusion.6
  872.3 2.3 fusion.12
  874.6 4.4 copy.53
  879.1 143.5 %reduce-scatter.8.cloned.1.call-done = f32[4,32,128]{2,1,0:T(8,128)} async-done(((f32[256,32,128]{2,1,0:T(8,128)}), f32[4,32,128]{2,1,0:T(8,128)}) %reduce-scatter.8.cloned.1.call-update) | async-done | bytes 65552 | tf_op jit(solution)/shard_map/reduce_scatter | solution.py:21
  1022.6 2.1 convolution_bitcast_fusion
  1024.8 0.1 constant_dynamic-slice_fusion
  1024.9 0.1 copy.57
  1025.0 0.1 constant_dynamic-slice_fusion.1
  1025.2 0.1 copy.56
  1025.3 0.1 constant_dynamic-slice_fusion.2
  1025.4 0.1 copy.55
  1025.5 45.5 %all-reduce.20.cloned.1.call-done = f32[4,128,128]{1,2,0:T(8,128)} async-done(((f32[4,128,128]{1,2,0:T(8,128)}), f32[4,128,128]{1,2,0:T(8,128)}) %all-reduce.20.cloned.1.call-update) | async-done | bytes 262160 | tf_op jit(solution)/shard_map/psum | solution.py:35
  1071.0 1.1 constant_dynamic-slice_fusion.3
  1072.1 0.1 copy.54
  1072.2 0.7 pad_maximum_fusion
  (41 shorter events, 0.5 us)
Async XLA Ops:
  6.5 84.4 %all-gather.4.cloned.1.call-start = ((), (), s32[]{:S(2)}) async-start(), calls=%async_computation.3 | async-start | bytes 4259840 | tf_op jit(solution)/shard_map/all_gather | solution.py:10
  8.5 137.1 %all-reduce.8.cloned.1.call-start = ((), (), s32[]{:S(2)}) async-start(), calls=%async_computation.4 | async-start | bytes 524288 | tf_op jit(solution)/shard_map/psum | solution.py:30
  13.2 87.1 %copy-start.5 = (f32[4,4,128,128]{3,2,1,0:T(8,128)S(1)}, f32[4,4,128,128]{3,2,1,0:T(8,128)}, u32[]{:S(2)}) copy-start(f32[4,4,128,128]{3,2,1,0:T(8,128)} %param.4) | copy-start | bytes 3145732
  91.0 6.2 copy-start.6
  97.2 48.4 %copy-start.4 = (f32[4,4,32,128]{3,2,1,0:T(8,128)S(1)}, f32[4,4,32,128]{3,2,1,0:T(8,128)}, u32[]{:S(2)}) copy-start(f32[4,4,32,128]{3,2,1,0:T(8,128)} %param.5) | copy-start | bytes 786436
  100.2 126.9 %all-gather.6.cloned.1.call-start = ((), (), s32[]{:S(2)}) async-start(), calls=%async_computation.5 | async-start | bytes 4259840 | tf_op jit(solution)/shard_map/all_gather | solution.py:10
  147.7 133.9 %all-reduce.10.cloned.1.call-start = ((), (), s32[]{:S(2)}) async-start(), calls=%async_computation.6 | async-start | bytes 524288 | tf_op jit(solution)/shard_map/psum | solution.py:30
  236.3 126.3 %all-gather.8.cloned.1.call-start = ((), (), s32[]{:S(2)}) async-start(), calls=%async_computation.7 | async-start | bytes 4259840 | tf_op jit(solution)/shard_map/all_gather | solution.py:10
  283.7 134.8 %all-reduce.12.cloned.1.call-start = ((), (), s32[]{:S(2)}) async-start(), calls=%async_computation.8 | async-start | bytes 524288 | tf_op jit(solution)/shard_map/psum | solution.py:30
  368.7 100.1 %copy-start = (f32[3,4,16,32,128]{4,3,2,1,0:T(8,128)S(1)}, f32[3,4,16,32,128]{4,3,2,1,0:T(8,128)}, u32[]{:S(2)}) copy-start(f32[3,4,16,32,128]{4,3,2,1,0:T(8,128)} %param.6) | copy-start | bytes 9437188
  373.1 95.7 %all-reduce.14.cloned.1.call-start = ((), (), s32[]{:S(2)}) async-start(), calls=%async_computation.9 | async-start | bytes 524288 | tf_op jit(solution)/shard_map/psum | solution.py:35
  421.4 199.7 %reduce-scatter.4.cloned.1.call-start = ((), (), s32[]{:S(2)}) async-start(), calls=%async_computation.10 | async-start | bytes 4259840 | tf_op jit(solution)/shard_map/reduce_scatter | solution.py:21
  477.5 143.6 %copy-start.8 = (f32[4,32,128]{2,1,0:T(8,128)S(1)}, f32[4,32,128]{2,1,0:T(8,128)}, u32[]{:S(2)}) copy-start(f32[4,32,128]{2,1,0:T(8,128)} %convolution_bitcast_fusion.7) | copy-start | bytes 196612
  477.5 192.0 %all-reduce.16.cloned.1.call-start = ((), (), s32[]{:S(2)}) async-start(), calls=%async_computation.11 | async-start | bytes 524288 | tf_op jit(solution)/shard_map/psum | solution.py:35
  623.3 198.6 %reduce-scatter.6.cloned.1.call-start = ((), (), s32[]{:S(2)}) async-start(), calls=%async_computation.12 | async-start | bytes 4259840 | tf_op jit(solution)/shard_map/reduce_scatter | solution.py:21
  678.2 143.6 %copy-start.7 = (f32[4,32,128]{2,1,0:T(8,128)S(1)}, f32[4,32,128]{2,1,0:T(8,128)}, u32[]{:S(2)}) copy-start(f32[4,32,128]{2,1,0:T(8,128)} %convolution_bitcast_fusion.8) | copy-start | bytes 196612
  678.3 192.0 %all-reduce.18.cloned.1.call-start = ((), (), s32[]{:S(2)}) async-start(), calls=%async_computation.13 | async-start | bytes 524288 | tf_op jit(solution)/shard_map/psum | solution.py:35
  824.0 198.6 %reduce-scatter.8.cloned.1.call-start = ((), (), s32[]{:S(2)}) async-start(), calls=%async_computation.14 | async-start | bytes 4259840 | tf_op jit(solution)/shard_map/reduce_scatter | solution.py:21
  879.0 143.6 %copy-start.9 = (f32[4,32,128]{2,1,0:T(8,128)S(1)}, f32[4,32,128]{2,1,0:T(8,128)}, u32[]{:S(2)}) copy-start(f32[4,32,128]{2,1,0:T(8,128)} %fusion.22) | copy-start | bytes 196612
  879.0 145.8 %copy-start.1 = (f32[4,128,128]{1,2,0:T(8,128)S(1)}, f32[4,128,128]{1,2,0:T(8,128)}, u32[]{:S(2)}) copy-start(f32[4,128,128]{1,2,0:T(8,128)} %all-reduce.14.cloned.1.call-done) | copy-start | bytes 786436
  879.0 146.0 %copy-start.2 = (f32[4,128,128]{1,2,0:T(8,128)S(1)}, f32[4,128,128]{1,2,0:T(8,128)}, u32[]{:S(2)}) copy-start(f32[4,128,128]{1,2,0:T(8,128)} %all-reduce.16.cloned.1.call-done) | copy-start | bytes 786436
  879.0 146.3 %copy-start.3 = (f32[4,128,128]{1,2,0:T(8,128)S(1)}, f32[4,128,128]{1,2,0:T(8,128)}, u32[]{:S(2)}) copy-start(f32[4,128,128]{1,2,0:T(8,128)} %all-reduce.18.cloned.1.call-done) | copy-start | bytes 786436
  879.0 192.0 %all-reduce.20.cloned.1.call-start = ((), (), s32[]{:S(2)}) async-start(), calls=%async_computation.15 | async-start | bytes 524288 | tf_op jit(solution)/shard_map/psum | solution.py:35
Sparse Core Ops, SparseCore 0:
  10.1 80.7 all-gather.3
  100.3 45.2 all-reduce.7
  148.7 78.3 all-gather.5
  236.4 45.1 all-reduce.9
  284.2 78.3 all-gather.7
  373.2 45.2 all-reduce.11
  421.5 47.2 all-reduce.13
  477.6 143.4 reduce-scatter.3
  623.6 45.9 all-reduce.15
  678.4 143.4 reduce-scatter.5
  824.3 45.9 all-reduce.17
  879.1 143.4 reduce-scatter.7
  1025.0 45.9 all-reduce.19
where the time goes:
time: 1090 us; the launch traced here: 1080 us
  waiting for transfers between devices  983 us (90%)
  matrix products  57.1 us (5%)
  local copies, waits for them, and re-layouts  22.8 us (2%)
  between operations  13.7 us (1%)
    reduce_scatter x3, waiting for transfers between devices, return_terms(): lax.psum_scatter(jnp.einsum('me,erk->mrk', owners, terms, precision=exact...  431 us
    all_gather x3, waiting for transfers between devices, fetch_blocks(): shard_rows = lax.all_gather(previous, 'row', axis=0, tiled=True)  235 us
    psum x4, waiting for transfers between devices, backward_solve(): return lax.psum(partial_value, 'col')  184 us
    psum x3, waiting for transfers between devices, forward_update(): return lax.psum(partial_value, 'col')  133 us
  transfers between devices with their start and end apart: 13, of which 13 were waited for; matrix products, arithmetic and copies ran while one was open for 1% of the time, Pallas kernels for 0%

commit v1 on v0

--- a/solution.py
+++ b/solution.py
@@ -7,7 +7,9 @@
 
 
 def fetch_blocks(previous, wanted):
-    shard_rows = lax.all_gather(previous, "row", axis=0, tiled=True)
+    shard_rows = jnp.concatenate(
+        lax.all_to_all(jnp.stack([previous] * lax.axis_size("row")), "row", 0, 0), axis=0
+    )
     chooser = (wanted[:, None] == jnp.arange(shard_rows.shape[0], dtype=jnp.int32)[None, :]).astype(
         jnp.float32
     )

time: 1090 us -> 1170 us (1.073)
  waiting for transfers between devices: 983 us -> 1030 us
  starting transfers between devices: 2.1 us -> 35.8 us
    all_to_all x0 -> x3, waiting for transfers between devices: none -> 285 us  [fetch_blocks(): lax.all_to_all(jnp.stack([previous] * lax.axis_size('row')), 'row', 0, 0)]
    all_gather x3 -> x0, waiting for transfers between devices: 235 us -> none  [fetch_blocks(): shard_rows = lax.all_gather(previous, 'row', axis=0, tiled=True)]
    all_to_all x0 -> x3, starting transfers between devices: none -> 33.9 us  [fetch_blocks(): lax.all_to_all(jnp.stack([previous] * lax.axis_size('row')), 'row', 0, 0)]
  transfers between devices with their start and end apart: 13 -> 13, of which waited for: 13 -> 13; matrix products, arithmetic and copies ran while one was open for 1% -> 0% of each run, Pallas kernels for 0% -> 0%
where the time goes in v1:
time: 1170 us; the launch traced here: 1160 us
  waiting for transfers between devices  1030 us (88%)
  matrix products  53.5 us (5%)
  starting transfers between devices  35.8 us (3%)
  local copies, waits for them, and re-layouts  26.2 us (2%)
  between operations  14.2 us (1%)
    reduce_scatter x3, waiting for transfers between devices, return_terms(): lax.psum_scatter(jnp.einsum('me,erk->mrk', owners, terms, precision=exact...  431 us
    all_to_all x3, waiting for transfers between devices, fetch_blocks(): lax.all_to_all(jnp.stack([previous] * lax.axis_size('row')), 'row', 0, 0)  285 us
    psum x4, waiting for transfers between devices, backward_solve(): return lax.psum(partial_value, 'col')  184 us
    psum x3, waiting for transfers between devices, forward_update(): return lax.psum(partial_value, 'col')  128 us
    all_to_all x3, starting transfers between devices, fetch_blocks(): lax.all_to_all(jnp.stack([previous] * lax.axis_size('row')), 'row', 0, 0)  33.9 us
  transfers between devices with their start and end apart: 13, of which 13 were waited for; matrix products, arithmetic and copies ran while one was open for 0% of the time, Pallas kernels for 0%

profile of v1, /device:TPU:2, one launch (start us, length us, event | category | flops | bytes accessed | tf_op | source)
XLA Modules:
  0.0 1158.2 jit_solution(10139087442771048965)
XLA Ops:
  6.5 1.3 fusion.22
  7.9 0.6 copy-done.8
  8.5 2.5 stack.16
  11.0 12.5 %all-to-all-start = ((f32[64,4,32,128]{3,2,1,0:T(8,128)}), f32[64,4,32,128]{3,2,1,0:T(8,128)}, u32[]{:S(2)}, u32[]{:S(2)}) async-start(f32[64,4,32,128]{3,2,1,0:T(8,128)} %stack.16), calls=%async_computation | async-start | bytes 8388608 | tf_op jit(solution)/shard_map/all_to_all | solution.py:11
  23.6 0.1 copy.14
  23.7 1.8 slice_bitcast_fusion
  25.5 94.1 %all-to-all-done = f32[64,4,32,128]{3,2,1,0:T(8,128)} async-done(((f32[64,4,32,128]{3,2,1,0:T(8,128)}), f32[64,4,32,128]{3,2,1,0:T(8,128)}, u32[]{:S(2)}, u32[]{:S(2)}) %all-to-all-start) | async-done | bytes 4194336 | tf_op jit(solution)/shard_map/all_to_all | solution.py:11
  119.6 6.2 fusion.4
  125.8 3.0 convolution_bitcast_fusion.6
  128.8 43.3 %all-reduce.8.cloned.1.call-done = f32[4,128,128]{2,1,0:T(8,128)} async-done(((f32[4,128,128]{2,1,0:T(8,128)}), f32[4,128,128]{2,1,0:T(8,128)}) %all-reduce.8.cloned.1.call-update) | async-done | bytes 262160 | tf_op jit(solution)/shard_map/psum | solution.py:32
  172.2 1.4 convolution_bitcast_fusion.8
  173.6 2.5 stack.17
  176.1 10.7 all-to-all-start.1
  186.8 0.6 all-reduce.10.cloned.1.call-start
  187.5 0.1 copy.16
  187.6 95.4 %all-to-all-done.1 = f32[64,4,32,128]{3,2,1,0:T(8,128)} async-done(((f32[64,4,32,128]{3,2,1,0:T(8,128)}), f32[64,4,32,128]{3,2,1,0:T(8,128)}, u32[]{:S(2)}, u32[]{:S(2)}) %all-to-all-start.1) | async-done | bytes 4194336 | tf_op jit(solution)/shard_map/all_to_all | solution.py:11
  282.9 6.2 fusion.2
  289.1 3.0 convolution_bitcast_fusion.5
  292.2 42.4 %all-reduce.10.cloned.1.call-done = f32[4,128,128]{2,1,0:T(8,128)} async-done(((f32[4,128,128]{2,1,0:T(8,128)}), f32[4,128,128]{2,1,0:T(8,128)}) %all-reduce.10.cloned.1.call-update) | async-done | bytes 262160 | tf_op jit(solution)/shard_map/psum | solution.py:32
  334.5 1.4 convolution_bitcast_fusion.7
  335.9 2.5 stack.18
  338.4 10.7 all-to-all-start.2
  349.2 0.2 all-reduce.12.cloned.1.call-start
  349.4 0.6 copy.18
  350.0 95.3 %all-to-all-done.2 = f32[64,4,32,128]{3,2,1,0:T(8,128)} async-done(((f32[64,4,32,128]{3,2,1,0:T(8,128)}), f32[64,4,32,128]{3,2,1,0:T(8,128)}, u32[]{:S(2)}, u32[]{:S(2)}) %all-to-all-start.2) | async-done | bytes 4194336 | tf_op jit(solution)/shard_map/all_to_all | solution.py:11
  445.3 6.2 fusion
  451.5 3.0 convolution_bitcast_fusion.4
  454.6 42.3 %all-reduce.12.cloned.1.call-done = f32[4,128,128]{2,1,0:T(8,128)} async-done(((f32[4,128,128]{2,1,0:T(8,128)}), f32[4,128,128]{2,1,0:T(8,128)}) %all-reduce.12.cloned.1.call-update) | async-done | bytes 262160 | tf_op jit(solution)/shard_map/psum | solution.py:32
  496.9 1.4 fusion.21
  498.3 1.3 convolution_bitcast_fusion.3
  499.6 0.3 reduce-scatter.4.cloned.1.call-start
  499.9 0.1 eq.157
  500.0 47.1 %all-reduce.14.cloned.1.call-done = f32[4,128,128]{1,2,0:T(8,128)} async-done(((f32[4,128,128]{1,2,0:T(8,128)}), f32[4,128,128]{1,2,0:T(8,128)}) %all-reduce.14.cloned.1.call-update) | async-done | bytes 262160 | tf_op jit(solution)/shard_map/psum | solution.py:37
  547.0 1.9 fusion.19
  549.0 2.3 fusion.10
  551.3 4.4 copy.47
  555.7 143.5 %reduce-scatter.4.cloned.1.call-done = f32[4,32,128]{2,1,0:T(8,128)} async-done(((f32[256,32,128]{2,1,0:T(8,128)}), f32[4,32,128]{2,1,0:T(8,128)}) %reduce-scatter.4.cloned.1.call-update) | async-done | bytes 65552 | tf_op jit(solution)/shard_map/reduce_scatter | solution.py:23
  699.2 2.1 convolution_bitcast_fusion.2
  701.4 0.3 reduce-scatter.6.cloned.1.call-start
  701.7 0.1 eq.148
  701.8 45.8 %all-reduce.16.cloned.1.call-done = f32[4,128,128]{1,2,0:T(8,128)} async-done(((f32[4,128,128]{1,2,0:T(8,128)}), f32[4,128,128]{1,2,0:T(8,128)}) %all-reduce.16.cloned.1.call-update) | async-done | bytes 262160 | tf_op jit(solution)/shard_map/psum | solution.py:37
  747.6 2.0 fusion.17
  749.5 2.3 fusion.8
  751.8 4.4 copy.50
  756.3 143.5 %reduce-scatter.6.cloned.1.call-done = f32[4,32,128]{2,1,0:T(8,128)} async-done(((f32[256,32,128]{2,1,0:T(8,128)}), f32[4,32,128]{2,1,0:T(8,128)}) %reduce-scatter.6.cloned.1.call-update) | async-done | bytes 65552 | tf_op jit(solution)/shard_map/reduce_scatter | solution.py:23
  899.8 2.1 convolution_bitcast_fusion.1
  902.0 0.3 reduce-scatter.8.cloned.1.call-start
  902.3 0.1 eq.139
  902.4 45.9 %all-reduce.18.cloned.1.call-done = f32[4,128,128]{1,2,0:T(8,128)} async-done(((f32[4,128,128]{1,2,0:T(8,128)}), f32[4,128,128]{1,2,0:T(8,128)}) %all-reduce.18.cloned.1.call-update) | async-done | bytes 262160 | tf_op jit(solution)/shard_map/psum | solution.py:37
  948.3 1.9 fusion.15
  950.3 2.3 fusion.6
  952.6 4.4 copy.53
  957.0 143.5 %reduce-scatter.8.cloned.1.call-done = f32[4,32,128]{2,1,0:T(8,128)} async-done(((f32[256,32,128]{2,1,0:T(8,128)}), f32[4,32,128]{2,1,0:T(8,128)}) %reduce-scatter.8.cloned.1.call-update) | async-done | bytes 65552 | tf_op jit(solution)/shard_map/reduce_scatter | solution.py:23
  1100.5 2.1 convolution_bitcast_fusion
  1102.7 0.1 constant_dynamic-slice_fusion
  1102.8 0.1 copy.26
  1102.9 0.1 constant_dynamic-slice_fusion.1
  1103.1 0.1 copy.25
  1103.2 0.1 constant_dynamic-slice_fusion.2
  1103.3 0.1 copy.24
  1103.4 45.5 %all-reduce.20.cloned.1.call-done = f32[4,128,128]{1,2,0:T(8,128)} async-done(((f32[4,128,128]{1,2,0:T(8,128)}), f32[4,128,128]{1,2,0:T(8,128)}) %all-reduce.20.cloned.1.call-update) | async-done | bytes 262160 | tf_op jit(solution)/shard_map/psum | solution.py:37
  1148.9 1.1 constant_dynamic-slice_fusion.3
  1150.0 0.1 copy.23
  1150.1 0.7 pad_maximum_fusion
  (41 shorter events, 0.6 us)
Async XLA Ops:
  7.9 0.6 copy-start.8
  11.0 12.5 %copy-start.10 = (s32[3,256,16]{1,2,0:T(8,128)S(1)}, s32[3,256,16]{1,2,0:T(8,128)}, u32[]{:S(2)}) copy-start(s32[3,256,16]{1,2,0:T(8,128)} %param.7) | copy-start | bytes 147460
  11.0 12.7 %copy-start = (f32[3,4,16,32,128]{4,3,2,1,0:T(8,128)S(1)}, f32[3,4,16,32,128]{4,3,2,1,0:T(8,128)}, u32[]{:S(2)}) copy-start(f32[3,4,16,32,128]{4,3,2,1,0:T(8,128)} %param.6) | copy-start | bytes 9437188
  11.0 108.6 %all-to-all-start = ((f32[64,4,32,128]{3,2,1,0:T(8,128)}), f32[64,4,32,128]{3,2,1,0:T(8,128)}, u32[]{:S(2)}, u32[]{:S(2)}) async-start(f32[64,4,32,128]{3,2,1,0:T(8,128)} %stack.16), calls=%async_computation | async-start | bytes 8388608 | tf_op jit(solution)/shard_map/all_to_all | solution.py:11
  23.5 148.7 %all-reduce.8.cloned.1.call-start = ((), (), s32[]{:S(2)}) async-start(), calls=%async_computation.6 | async-start | bytes 524288 | tf_op jit(solution)/shard_map/psum | solution.py:32
  25.5 146.7 %copy-start.7 = (f32[4,4,32,128]{3,2,1,0:T(8,128)S(1)}, f32[4,4,32,128]{3,2,1,0:T(8,128)}, u32[]{:S(2)}) copy-start(f32[4,4,32,128]{3,2,1,0:T(8,128)} %param.5) | copy-start | bytes 786436
  119.6 6.2 copy-start.3
  176.1 106.9 %all-to-all-start.1 = ((f32[64,4,32,128]{3,2,1,0:T(8,128)}), f32[64,4,32,128]{3,2,1,0:T(8,128)}, u32[]{:S(2)}, u32[]{:S(2)}) async-start(f32[64,4,32,128]{3,2,1,0:T(8,128)} %stack.17), calls=%async_computation.1 | async-start | bytes 8388608 | tf_op jit(solution)/shard_map/all_to_all | solution.py:11
  186.8 147.7 %all-reduce.10.cloned.1.call-start = ((), (), s32[]{:S(2)}) async-start(), calls=%async_computation.7 | async-start | bytes 524288 | tf_op jit(solution)/shard_map/psum | solution.py:32
  282.9 6.2 copy-start.2
  338.4 106.9 %all-to-all-start.2 = ((f32[64,4,32,128]{3,2,1,0:T(8,128)}), f32[64,4,32,128]{3,2,1,0:T(8,128)}, u32[]{:S(2)}, u32[]{:S(2)}) async-start(f32[64,4,32,128]{3,2,1,0:T(8,128)} %stack.18), calls=%async_computation.2 | async-start | bytes 8388608 | tf_op jit(solution)/shard_map/all_to_all | solution.py:11
  349.2 147.7 %all-reduce.12.cloned.1.call-start = ((), (), s32[]{:S(2)}) async-start(), calls=%async_computation.8 | async-start | bytes 524288 | tf_op jit(solution)/shard_map/psum | solution.py:32
  445.3 6.2 copy-start.1
  445.3 54.6 %copy-start.11 = (s32[1,4,16]{2,1,0:T(4,128)S(1)}, s32[1,4,16]{2,1,0:T(4,128)}, u32[]{:S(2)}) copy-start(s32[1,4,16]{2,1,0:T(4,128)} %copy.18) | copy-start | bytes 772
  454.6 92.5 %all-reduce.14.cloned.1.call-start = ((), (), s32[]{:S(2)}) async-start(), calls=%async_computation.9 | async-start | bytes 524288 | tf_op jit(solution)/shard_map/psum | solution.py:37
  499.6 199.6 %reduce-scatter.4.cloned.1.call-start = ((), (), s32[]{:S(2)}) async-start(), calls=%async_computation.10 | async-start | bytes 4259840 | tf_op jit(solution)/shard_map/reduce_scatter | solution.py:23
  555.7 191.9 %all-reduce.16.cloned.1.call-start = ((), (), s32[]{:S(2)}) async-start(), calls=%async_computation.11 | async-start | bytes 524288 | tf_op jit(solution)/shard_map/psum | solution.py:37
  701.4 198.4 %reduce-scatter.6.cloned.1.call-start = ((), (), s32[]{:S(2)}) async-start(), calls=%async_computation.12 | async-start | bytes 4259840 | tf_op jit(solution)/shard_map/reduce_scatter | solution.py:23
  756.2 192.1 %all-reduce.18.cloned.1.call-start = ((), (), s32[]{:S(2)}) async-start(), calls=%async_computation.13 | async-start | bytes 524288 | tf_op jit(solution)/shard_map/psum | solution.py:37
  902.0 198.5 %reduce-scatter.8.cloned.1.call-start = ((), (), s32[]{:S(2)}) async-start(), calls=%async_computation.14 | async-start | bytes 4259840 | tf_op jit(solution)/shard_map/reduce_scatter | solution.py:23
  956.9 143.6 %copy-start.9 = (f32[4,32,128]{2,1,0:T(8,128)S(1)}, f32[4,32,128]{2,1,0:T(8,128)}, u32[]{:S(2)}) copy-start(f32[4,32,128]{2,1,0:T(8,128)} %copy-done.8) | copy-start | bytes 196612
  956.9 145.8 %copy-start.4 = (f32[4,128,128]{1,2,0:T(8,128)S(1)}, f32[4,128,128]{1,2,0:T(8,128)}, u32[]{:S(2)}) copy-start(f32[4,128,128]{1,2,0:T(8,128)} %all-reduce.14.cloned.1.call-done) | copy-start | bytes 786436
  956.9 146.0 %copy-start.5 = (f32[4,128,128]{1,2,0:T(8,128)S(1)}, f32[4,128,128]{1,2,0:T(8,128)}, u32[]{:S(2)}) copy-start(f32[4,128,128]{1,2,0:T(8,128)} %all-reduce.16.cloned.1.call-done) | copy-start | bytes 786436
  956.9 146.3 %copy-start.6 = (f32[4,128,128]{1,2,0:T(8,128)S(1)}, f32[4,128,128]{1,2,0:T(8,128)}, u32[]{:S(2)}) copy-start(f32[4,128,128]{1,2,0:T(8,128)} %all-reduce.18.cloned.1.call-done) | copy-start | bytes 786436
  957.0 191.9 %all-reduce.20.cloned.1.call-start = ((), (), s32[]{:S(2)}) async-start(), calls=%async_computation.15 | async-start | bytes 524288 | tf_op jit(solution)/shard_map/psum | solution.py:37
Sparse Core Ops, SparseCore 0:
  129.0 43.1 all-reduce.7
  292.3 42.1 all-reduce.9
  454.7 42.1 all-reduce.11
  499.7 47.2 all-reduce.13
  555.8 143.3 reduce-scatter.3
  701.5 46.0 all-reduce.15
  756.3 143.4 reduce-scatter.5
  902.2 46.0 all-reduce.17
  957.1 143.3 reduce-scatter.7
  1102.8 46.0 all-reduce.19
